TPU v7x, 256 devices: a whole 4x4x8 slice. The times are simulated.
256 devices in a mesh: dp: 4 (over x), space: 16 (over z_lo, y), tm: 4 (over z_hi, core).
Axes of the slice: x: 4, y: 4, z: 8 (z_hi: 2, z_lo: 4; z = z_hi * 4 + z_lo), core: 2. Of those that a mesh axis runs over, the one named last changes fastest.
Arguments:
- inputs: bfloat16 [4, 32, 64, 4096], P('dp', 'tm', None, 'space'), may hold values from -6 to 6
- grad_out: bfloat16 [4, 32, 64, 4096], P('dp', 'tm', None, 'space'), may hold values from -6 to 6
- conv_w: bfloat16 [2, 128, 64], replicated, may hold values from -0.5 to 0.5
- conv_b: float32 [128], replicated, may hold values from -3 to 3
- mix_w: bfloat16 [3, 64, 64], replicated, may hold values from -0.4375 to 0.4375
- mix_b: float32 [64], replicated, may hold values from -3 to 3
- adj_tiles: bfloat16 [32, 8, 128, 128], P('space'), may hold values from -0.1875 to 0.1875
- tile_cols: int32 [32, 8], P('space'), may hold values from 0 to 9, as said below
- send_rows: int32 [16, 16, 64], P('space'), may hold values from 0 to 255
- counts: int32 [16, 16], P('space'), may hold values from 0 to 64, as said below
Outputs:
- outputs: bfloat16 [4, 32, 64, 4096], P('dp', 'tm', None, 'space')
- grad_inputs: bfloat16 [4, 32, 64, 4096], P('dp', 'tm', None, 'space')
- grad_conv_w: float32 [2, 128, 64], replicated
- grad_conv_b: float32 [128], replicated
- grad_mix_w: float32 [3, 64, 64], replicated
- grad_mix_b: float32 [64], replicated
Inputs may be any that keep to these rules, and one draw needn't show every extreme that they name: counts[s, s] = 0; counts[0, 1] = 64. `tile_cols`: column blocks below 2 are the part's own sensor blocks, 2 + i the i-th block of 128 received slots in order of source part and slot; in each row block the first 4 ids are below 2, the others are not.
All inputs are finite; a program needn't handle non-finite values.
Results may differ from a plain program's by a relative error of at most 0.0058.
Values may be sent and summed in bfloat16 or wider, within the bound.
A program may use at most 64 MiB of HBM per device.

v0:
```python
import math
import jax
import jax.numpy as jnp
from jax import lax
from jax.sharding import PartitionSpec as P

DILATION_SIZE = 2


def from_behind(value, axis, steps):
    count = lax.axis_size(axis)
    leading, last = (max(0, -steps), min(count, count - steps))
    return lax.ppermute(value, axis, [(source, source + steps) for source in range(leading, last)])


def slot_mask(counts, slot_count, dtype):
    slots = lax.broadcasted_iota(jnp.int32, (counts.shape[1], slot_count), 1)
    return (slots < counts[0][:, None]).astype(dtype)


def pack_rows(field, send_rows, live_slots):
    picked = field[:, :, send_rows[0]] * live_slots
    return picked.reshape(field.shape[0], field.shape[1], -1)


def tile_product(extended, adj_tiles, tile_cols):
    timestep_count, chan_count = (extended.shape[0], extended.shape[1])
    blocks = extended.reshape(timestep_count, chan_count, -1, adj_tiles.shape[2])
    picked = blocks[:, :, tile_cols]
    return jnp.einsum("tcrkj,rkij->tcri", picked, adj_tiles, preferred_element_type=jnp.float32)


def forward_start(field, send_rows, live_slots):
    packed = pack_rows(field, send_rows, live_slots)
    own_part = None
    return (packed, own_part)


def forward_finish(field, received, adj_tiles, tile_cols):
    total = tile_product(jnp.concatenate([field, received], 2), adj_tiles, tile_cols)
    return total.reshape(field.shape).astype(jnp.bfloat16)


def back_start(grad, adj_tiles, tile_cols, send_rows):
    timestep_count, chan_count, sensor_count = grad.shape
    tile_size = adj_tiles.shape[2]
    row_blocks = sensor_count // tile_size
    half_slots = tile_cols.shape[1] // 2
    halo_blocks = send_rows.shape[1] * send_rows.shape[2] // tile_size
    blocks = grad.reshape(timestep_count, chan_count, row_blocks, tile_size)
    remote_terms = jnp.einsum(
        "tcri,rkij->tcrkj", blocks, adj_tiles[:, half_slots:], preferred_element_type=jnp.float32
    )
    remote_sums = jnp.zeros((timestep_count, chan_count, halo_blocks, tile_size), jnp.float32)
    remote_sums = remote_sums.at[:, :, tile_cols[:, half_slots:] - row_blocks].add(remote_terms)
    return remote_sums.reshape(timestep_count, chan_count, -1).astype(jnp.bfloat16)


def back_finish(grad, returned, adj_tiles, tile_cols, send_rows, live_slots):
    timestep_count, chan_count, sensor_count = grad.shape
    tile_size = adj_tiles.shape[2]
    row_blocks = sensor_count // tile_size
    half_slots = tile_cols.shape[1] // 2
    blocks = grad.reshape(timestep_count, chan_count, row_blocks, tile_size)
    own_terms = jnp.einsum(
        "tcri,rkij->tcrkj", blocks, adj_tiles[:, :half_slots], preferred_element_type=jnp.float32
    )
    total = jnp.zeros((timestep_count, chan_count, row_blocks, tile_size), jnp.float32)
    total = total.at[:, :, tile_cols[:, :half_slots]].add(own_terms).reshape(grad.shape)
    returned = returned.reshape(
        timestep_count, chan_count, send_rows.shape[1], send_rows.shape[2]
    ).astype(jnp.float32)
    return total.at[:, :, send_rows[0]].add(returned * live_slots.astype(jnp.float32))


def mixing_grads(sample_grad, fields):
    grad_mix_w = jnp.stack(
        [
            jnp.einsum("ton,tcn->oc", sample_grad, item, preferred_element_type=jnp.float32)
            for item in fields
        ]
    )
    grad_mix_b = jnp.sum(sample_grad.astype(jnp.float32), axis=(0, 2))
    return (grad_mix_w, grad_mix_b)


def body(inputs, grad_out, conv_w, conv_b, mix_w, mix_b, adj_tiles, tile_cols, send_rows, counts):
    sample_input = inputs[0]
    sample_grad = grad_out[0]
    timestep_count, chan_count, sensor_count = sample_input.shape
    live_slots = slot_mask(counts, send_rows.shape[2], jnp.bfloat16)
    prior_border_slice = from_behind(sample_input[timestep_count - DILATION_SIZE :], "tm", 1)
    preceding_window = jnp.concatenate(
        [prior_border_slice, sample_input[: timestep_count - DILATION_SIZE]], 0
    )
    preact = jnp.einsum("oc,tcn->ton", conv_w[1], sample_input, preferred_element_type=jnp.float32)
    preact = preact + jnp.einsum(
        "oc,tcn->ton", conv_w[0], preceding_window, preferred_element_type=jnp.float32
    )
    preact = preact + conv_b[None, :, None]
    filtered = jnp.tanh(preact[:, :chan_count])
    gating = jax.nn.sigmoid(preact[:, chan_count:])
    hidden = (filtered * gating).astype(jnp.bfloat16)
    grad_float = sample_grad.astype(jnp.float32)
    packed_one, early_one = forward_start(hidden, send_rows, live_slots)
    received_one = lax.all_to_all(packed_one, "space", split_axis=2, concat_axis=2, tiled=True)
    hop_one = forward_finish(hidden, received_one, adj_tiles, tile_cols)
    packed_two, early_two = forward_start(hop_one, send_rows, live_slots)
    received_two = lax.all_to_all(packed_two, "space", split_axis=2, concat_axis=2, tiled=True)
    hop_two = forward_finish(hop_one, received_two, adj_tiles, tile_cols)
    fields = (hidden, hop_one, hop_two)
    grad_mix_w, grad_mix_b = mixing_grads(sample_grad, fields)
    back_two = jnp.einsum(
        "oc,ton->tcn", mix_w[2], sample_grad, preferred_element_type=jnp.float32
    ).astype(jnp.bfloat16)
    returned_two = lax.all_to_all(
        back_start(back_two, adj_tiles, tile_cols, send_rows),
        "space",
        split_axis=2,
        concat_axis=2,
        tiled=True,
    )
    back_one = jnp.einsum("oc,ton->tcn", mix_w[1], sample_grad, preferred_element_type=jnp.float32)
    back_one = (
        back_one + back_finish(back_two, returned_two, adj_tiles, tile_cols, send_rows, live_slots)
    ).astype(jnp.bfloat16)
    returned_one = lax.all_to_all(
        back_start(back_one, adj_tiles, tile_cols, send_rows),
        "space",
        split_axis=2,
        concat_axis=2,
        tiled=True,
    )
    back_hidden = jnp.einsum(
        "oc,ton->tcn", mix_w[0], sample_grad, preferred_element_type=jnp.float32
    )
    back_hidden = back_hidden + back_finish(
        back_one, returned_one, adj_tiles, tile_cols, send_rows, live_slots
    )
    mixed = sample_input.astype(jnp.float32) + mix_b[None, :, None]
    for index in range(3):
        mixed = mixed + jnp.einsum(
            "oc,tcn->ton", mix_w[index], fields[index], preferred_element_type=jnp.float32
        )
    outputs = mixed.astype(jnp.bfloat16)[None]
    grad_filter = back_hidden * (1.0 - filtered * filtered) * gating
    grad_gate = back_hidden * filtered * gating * (1.0 - gating)
    backward_preactivation = jnp.concatenate([grad_filter, grad_gate], 1).astype(jnp.bfloat16)
    next_border_slice = from_behind(backward_preactivation[:DILATION_SIZE], "tm", -1)
    following_window = jnp.concatenate(
        [backward_preactivation[DILATION_SIZE:], next_border_slice], 0
    )
    grad_inputs = grad_float + jnp.einsum(
        "oc,ton->tcn", conv_w[1], backward_preactivation, preferred_element_type=jnp.float32
    )
    grad_inputs = grad_inputs + jnp.einsum(
        "oc,ton->tcn", conv_w[0], following_window, preferred_element_type=jnp.float32
    )
    grad_inputs = grad_inputs.astype(jnp.bfloat16)[None]
    grad_conv_w = jnp.stack(
        [
            jnp.einsum(
                "ton,tcn->oc",
                backward_preactivation,
                preceding_window,
                preferred_element_type=jnp.float32,
            ),
            jnp.einsum(
                "ton,tcn->oc",
                backward_preactivation,
                sample_input,
                preferred_element_type=jnp.float32,
            ),
        ]
    )
    grad_conv_b = jnp.sum(backward_preactivation.astype(jnp.float32), axis=(0, 2))
    grad_conv_w, grad_conv_b, grad_mix_w, grad_mix_b = lax.psum(
        (grad_conv_w, grad_conv_b, grad_mix_w, grad_mix_b), ("dp", "space", "tm")
    )
    cell_count = (
        inputs.shape[0]
        * timestep_count
        * sensor_count
        * lax.axis_size("dp")
        * lax.axis_size("space")
        * lax.axis_size("tm")
    )
    scale = 1.0 / math.sqrt(cell_count)
    return (
        outputs,
        grad_inputs,
        grad_conv_w * scale,
        grad_conv_b * scale,
        grad_mix_w * scale,
        grad_mix_b * scale,
    )


def solution(mesh):
    in_specs = (
        P("dp", "tm", None, "space"),
        P("dp", "tm", None, "space"),
        P(),
        P(),
        P(),
        P(),
        P("space", None, None, None),
        P("space", None),
        P("space", None, None),
        P("space", None),
    )
    out_specs = (P("dp", "tm", None, "space"), P("dp", "tm", None, "space"), P(), P(), P(), P())
    return jax.shard_map(body, mesh=mesh, in_specs=in_specs, out_specs=out_specs, check_vma=False)
```

profile of v0, /device:TPU:1, one launch (start us, length us, event | category | flops | bytes accessed | tf_op | source)
XLA Modules:
  0.0 680.7 jit_solution(10881315894750508709)
XLA Ops:
  12.5 3.5 scatter_fusion.1
  19.6 9.2 %all-to-all-start.2 = ((bf16[16,2,16384]{2,1,0:T(2,128)(2,1)}), bf16[16,2,16384]{2,1,0:T(2,128)(2,1)}, u32[]{:S(2)}, u32[]{:S(2)}) async-start(bf16[16,2,16384]{2,1,0:T(2,128)(2,1)} %reshape.258), calls=%async_computation.2 | async-start | bytes 2097152 | tf_op jit(solution)/shard_map/all_to_all | solution.py:116
  32.5 18.7 %all-to-all-done.2 = bf16[16,2,16384]{2,1,0:T(2,128)(2,1)} async-done(((bf16[16,2,16384]{2,1,0:T(2,128)(2,1)}), bf16[16,2,16384]{2,1,0:T(2,128)(2,1)}, u32[]{:S(2)}, u32[]{:S(2)}) %all-to-all-start.2) | async-done | bytes 1048608 | tf_op jit(solution)/shard_map/all_to_all | solution.py:116
  51.2 3.8 reshape.259
  55.0 3.1 convert_multiply_fusion.1
  58.1 71.3 %scatter_fusion.2 = f32[8,64,256]{1,0,2:T(8,128)S(1)} fusion(f32[8,64,256]{1,0,2:T(8,128)S(1)} %copy.84, s32[1024]{0:T(1024)S(1)} %reshape.131, f32[1024,8,64]{2,1,0:T(8,128)} %bitcast.273), kind=kCustom, calls=%fused_computation.6 | custom fusion | flops 524288 | bytes 6295552 | tf_op jit(solution)/shard_map/scatter-add | solution.py:73
  132.5 3.5 scatter_fusion.4
  141.6 7.7 %all-to-all-start.3 = ((bf16[16,2,16384]{2,1,0:T(2,128)(2,1)}), bf16[16,2,16384]{2,1,0:T(2,128)(2,1)}, u32[]{:S(2)}, u32[]{:S(2)}) async-start(bf16[16,2,16384]{2,1,0:T(2,128)(2,1)} %reshape.260), calls=%async_computation.3 | async-start | bytes 2097152 | tf_op jit(solution)/shard_map/all_to_all | solution.py:127
  149.3 8.2 %collective-permute-start = (bf16[2,64,256]{2,1,0:T(8,128)(2,1)S(1)}, bf16[2,64,256]{2,1,0:T(8,128)(2,1)S(1)}, u32[]{:S(2)}, u32[]{:S(2)}) collective-permute-start(bf16[2,64,256]{2,1,0:T(8,128)(2,1)S(1)} %slice_bitcast_fusion.1), channel_id=1, source_target_pairs={{0,1},{1,2},{2,3},{4,5},{5,6},{6,7},{8,9},{9,10},{10,11},{12,13},{... | collective-permute-start | bytes 196616 | tf_op jit(solution)/shard_map/ppermute | solution.py:13
  158.2 7.7 %collective-permute-done = bf16[2,64,256]{2,1,0:T(8,128)(2,1)S(1)} collective-permute-done((bf16[2,64,256]{2,1,0:T(8,128)(2,1)S(1)}, bf16[2,64,256]{2,1,0:T(8,128)(2,1)S(1)}, u32[]{:S(2)}, u32[]{:S(2)}) %collective-permute-start) | collective-permute-done | bytes 65568 | tf_op jit(solution)/shard_map/ppermute | solution.py:13
  172.2 3.8 reshape.261
  175.9 3.1 convert_multiply_fusion
  179.0 71.3 %scatter_fusion.5 = f32[8,64,256]{1,0,2:T(8,128)S(1)} fusion(f32[8,64,256]{1,0,2:T(8,128)S(1)} %copy.92, s32[1024]{0:T(1024)S(1)} %reshape.131, f32[1024,8,64]{2,1,0:T(8,128)} %bitcast.272), kind=kCustom, calls=%fused_computation.9 | custom fusion | flops 524288 | bytes 6295552 | tf_op jit(solution)/shard_map/scatter-add | solution.py:73
  252.6 7.6 %gather_fusion = bf16[1024,8,64]{2,1,0:T(8,128)(2,1)} fusion(bf16[8,64,256]{1,0,2:T(8,128)(2,1)S(1)} %copy.63, s32[1024]{0:T(1024)S(1)} %broadcast_clamp_fusion), kind=kCustom, calls=%fused_computation | custom fusion | bytes 2101248 | tf_op jit(solution)/shard_map/gather | solution.py:22
  260.1 4.9 fusion.76
  267.3 7.9 %all-to-all-start = ((bf16[16,2,16384]{2,1,0:T(2,128)(2,1)}), bf16[16,2,16384]{2,1,0:T(2,128)(2,1)S(1)}, u32[]{:S(2)}, u32[]{:S(2)}) async-start(bf16[16,2,16384]{2,1,0:T(2,128)(2,1)} %reshape.254), calls=%async_computation | async-start | bytes 2097152 | tf_op jit(solution)/shard_map/all_to_all | solution.py:106
  276.1 21.2 %all-to-all-done = bf16[16,2,16384]{2,1,0:T(2,128)(2,1)S(1)} async-done(((bf16[16,2,16384]{2,1,0:T(2,128)(2,1)}), bf16[16,2,16384]{2,1,0:T(2,128)(2,1)S(1)}, u32[]{:S(2)}, u32[]{:S(2)}) %all-to-all-start) | async-done | bytes 1048608 | tf_op jit(solution)/shard_map/all_to_all | solution.py:106
  297.3 2.3 reshape.255
  299.7 3.4 pad_maximum_fusion
  303.1 3.4 copy.65
  306.5 2.3 gather_fusion.1
  309.9 3.3 gather_fusion.2
  313.2 4.8 fusion.77
  318.0 4.7 reshape.256
  322.7 7.9 %all-to-all-start.1 = ((bf16[16,2,16384]{2,1,0:T(2,128)(2,1)}), bf16[16,2,16384]{2,1,0:T(2,128)(2,1)S(1)}, u32[]{:S(2)}, u32[]{:S(2)}) async-start(bf16[16,2,16384]{2,1,0:T(2,128)(2,1)} %reshape.256), calls=%async_computation.1 | async-start | bytes 2097152 | tf_op jit(solution)/shard_map/all_to_all | solution.py:109
  336.4 4.1 collective-permute-start.1
  340.7 236.7 %all-reduce.3.cloned.1.call-done = f32[2,128,64]{1,2,0:T(8,128)} async-done(((f32[2,128,64]{1,2,0:T(8,128)}), f32[2,128,64]{1,2,0:T(8,128)}) %all-reduce.3.cloned.1.call-update) | async-done | bytes 65552 | tf_op jit(solution)/shard_map/psum | solution.py:177
  582.9 2.3 reshape.257
  585.3 3.4 pad_maximum_fusion.1
  588.7 3.4 copy.71
  592.1 2.3 gather_fusion.3
  597.1 75.0 %all-reduce = (f32[128]{0:T(128)S(1)}, f32[3,64,64]{1,2,0:T(8,128)S(1)}, f32[64]{0:T(128)S(1)}) all-reduce(f32[128]{0:T(128)S(1)} %convert_reduce_fusion, f32[3,64,64]{1,2,0:T(8,128)S(1)} %pad_maximum_fusion.6, f32[64]{0:T(128)S(1)} %convert_reduce_fusion.1), channel_id=1, replica_groups=mesh['dp'=4,'space'=16,'tm'=4] {'dp','space','tm'}, use_global_device_ids=true, to_apply=%region_8.0 | all-reduce | flops 12480 | bytes 99840 | tf_op jit(solution)/shard_map/psum | solution.py:177
  (135 shorter events, 50.1 us)
Async XLA Ops:
  17.3 11.6 %copy-start.1 = (bf16[2,8,128,128]{3,2,1,0:T(8,128)(2,1)S(1)}, bf16[2,8,128,128]{3,2,1,0:T(8,128)(2,1)}, u32[]{:S(2)}) copy-start(bf16[2,8,128,128]{3,2,1,0:T(8,128)(2,1)} %param.16) | copy-start | bytes 1572868
  19.6 31.6 %all-to-all-start.2 = ((bf16[16,2,16384]{2,1,0:T(2,128)(2,1)}), bf16[16,2,16384]{2,1,0:T(2,128)(2,1)}, u32[]{:S(2)}, u32[]{:S(2)}) async-start(bf16[16,2,16384]{2,1,0:T(2,128)(2,1)} %reshape.258), calls=%async_computation.2 | async-start | bytes 2097152 | tf_op jit(solution)/shard_map/all_to_all | solution.py:116
  29.7 1.9 copy-start
  29.7 1.9 copy-start.19
  31.6 0.8 copy-start.24
  129.3 1.0 copy-start.2
  139.3 10.0 %copy-start.12 = (bf16[1,8,64,256]{3,2,1,0:T(8,128)(2,1)S(1)}, bf16[1,8,64,256]{3,2,1,0:T(8,128)(2,1)}, u32[]{:S(2)}) copy-start(bf16[1,8,64,256]{3,2,1,0:T(8,128)(2,1)} %param.10) | copy-start | bytes 786436
  141.6 16.3 %copy-start.21 = (bf16[2,128,64]{1,2,0:T(8,128)(2,1)S(1)}, bf16[2,128,64]{1,2,0:T(8,128)(2,1)}, u32[]{:S(2)}) copy-start(bf16[2,128,64]{1,2,0:T(8,128)(2,1)} %param.12) | copy-start | bytes 98308
  141.6 24.3 %copy-start.26 = (f32[128]{0:T(128)S(1)}, f32[128]{0:T(128)}, u32[]{:S(2)}) copy-start(f32[128]{0:T(128)} %param.13) | copy-start | bytes 1540
  141.6 30.6 %all-to-all-start.3 = ((bf16[16,2,16384]{2,1,0:T(2,128)(2,1)}), bf16[16,2,16384]{2,1,0:T(2,128)(2,1)}, u32[]{:S(2)}, u32[]{:S(2)}) async-start(bf16[16,2,16384]{2,1,0:T(2,128)(2,1)} %reshape.260), calls=%async_computation.3 | async-start | bytes 2097152 | tf_op jit(solution)/shard_map/all_to_all | solution.py:127
  149.3 16.6 %collective-permute-start = (bf16[2,64,256]{2,1,0:T(8,128)(2,1)S(1)}, bf16[2,64,256]{2,1,0:T(8,128)(2,1)S(1)}, u32[]{:S(2)}, u32[]{:S(2)}) collective-permute-start(bf16[2,64,256]{2,1,0:T(8,128)(2,1)S(1)} %slice_bitcast_fusion.1), channel_id=1, source_target_pairs={{0,1},{1,2},{2,3},{4,5},{5,6},{6,7},{8,9},{9,10},{10,11},{12,13},{... | collective-permute-start | bytes 196616 | tf_op jit(solution)/shard_map/ppermute | solution.py:13
  157.8 8.1 %copy-start.17 = (bf16[6,64,256]{2,1,0:T(8,128)(2,1)}, bf16[6,64,256]{2,1,0:T(8,128)(2,1)S(1)}, u32[]{:S(2)}) copy-start(bf16[6,64,256]{2,1,0:T(8,128)(2,1)S(1)} %slice_bitcast_fusion) | copy-start | bytes 589828
  250.3 1.2 copy-start.11
  251.9 23.9 %copy-start.5 = (bf16[8,64,256]{2,1,0:T(8,128)(2,1)}, bf16[8,64,256]{2,1,0:T(8,128)(2,1)S(1)}, u32[]{:S(2)}) copy-start(bf16[8,64,256]{2,1,0:T(8,128)(2,1)S(1)} %get-tuple-element.27) | copy-start | bytes 786436
  251.9 23.9 %copy-start.7 = (bf16[8,64,256]{2,1,0:T(8,128)(2,1)}, bf16[8,64,256]{2,1,0:T(8,128)(2,1)S(1)}, u32[]{:S(2)}) copy-start(bf16[8,64,256]{2,1,0:T(8,128)(2,1)S(1)} %get-tuple-element.28) | copy-start | bytes 786436
  265.1 10.2 %copy-start.22 = (s32[2,8]{1,0:T(2,128)S(1)}, s32[2,8]{1,0:T(2,128)}, u32[]{:S(2)}) copy-start(s32[2,8]{1,0:T(2,128)} %param.17) | copy-start | bytes 196
  267.3 8.2 %copy-start.18 = (bf16[6,64,256]{2,1,0:T(8,128)(2,1)S(1)}, bf16[6,64,256]{2,1,0:T(8,128)(2,1)}, u32[]{:S(2)}) copy-start(bf16[6,64,256]{2,1,0:T(8,128)(2,1)} %copy-done.17) | copy-start | bytes 589828
  267.3 8.5 %copy-start.13 = (bf16[1,8,64,256]{3,2,1,0:T(8,128)(2,1)S(1)}, bf16[1,8,64,256]{3,2,1,0:T(8,128)(2,1)}, u32[]{:S(2)}) copy-start(bf16[1,8,64,256]{3,2,1,0:T(8,128)(2,1)} %param.10) | copy-start | bytes 786436
  267.3 30.0 %all-to-all-start = ((bf16[16,2,16384]{2,1,0:T(2,128)(2,1)}), bf16[16,2,16384]{2,1,0:T(2,128)(2,1)S(1)}, u32[]{:S(2)}, u32[]{:S(2)}) async-start(bf16[16,2,16384]{2,1,0:T(2,128)(2,1)} %reshape.254), calls=%async_computation | async-start | bytes 2097152 | tf_op jit(solution)/shard_map/all_to_all | solution.py:106
  306.5 2.3 copy-start.3
  318.0 13.4 %copy-start.6 = (bf16[8,64,256]{2,1,0:T(8,128)(2,1)S(1)}, bf16[8,64,256]{2,1,0:T(8,128)(2,1)}, u32[]{:S(2)}) copy-start(bf16[8,64,256]{2,1,0:T(8,128)(2,1)} %copy-done.5) | copy-start | bytes 786436
  318.0 13.4 %copy-start.8 = (bf16[8,64,256]{2,1,0:T(8,128)(2,1)S(1)}, bf16[8,64,256]{2,1,0:T(8,128)(2,1)}, u32[]{:S(2)}) copy-start(bf16[8,64,256]{2,1,0:T(8,128)(2,1)} %copy-done.7) | copy-start | bytes 786436
  322.7 8.7 %copy-start.10 = (bf16[8,64,256]{2,1,0:T(8,128)(2,1)S(1)}, bf16[8,64,256]{2,1,0:T(8,128)(2,1)}, u32[]{:S(2)}) copy-start(bf16[8,64,256]{2,1,0:T(8,128)(2,1)} %copy-done.9) | copy-start | bytes 786436
  322.7 11.3 %copy-start.14 = (bf16[1,8,64,256]{3,2,1,0:T(8,128)(2,1)S(1)}, bf16[1,8,64,256]{3,2,1,0:T(8,128)(2,1)}, u32[]{:S(2)}) copy-start(bf16[1,8,64,256]{3,2,1,0:T(8,128)(2,1)} %param.10) | copy-start | bytes 786436
  322.7 11.3 %copy-start.25 = (f32[64]{0:T(128)S(1)}, f32[64]{0:T(128)}, u32[]{:S(2)}) copy-start(f32[64]{0:T(128)} %param.15) | copy-start | bytes 772
  322.7 260.2 %all-to-all-start.1 = ((bf16[16,2,16384]{2,1,0:T(2,128)(2,1)}), bf16[16,2,16384]{2,1,0:T(2,128)(2,1)S(1)}, u32[]{:S(2)}, u32[]{:S(2)}) async-start(bf16[16,2,16384]{2,1,0:T(2,128)(2,1)} %reshape.256), calls=%async_computation.1 | async-start | bytes 2097152 | tf_op jit(solution)/shard_map/all_to_all | solution.py:109
  330.6 246.8 %all-reduce.3.cloned.1.call-start = ((), (), s32[]{:S(2)}) async-start(), calls=%async_computation.4 | async-start | bytes 131072 | tf_op jit(solution)/shard_map/psum | solution.py:177
  335.7 245.5 %copy-start.16 = (f32[8,64,256]{2,1,0:T(8,128)S(1)}, f32[8,64,256]{2,1,0:T(8,128)}, u32[]{:S(2)}) copy-start(f32[8,64,256]{2,1,0:T(8,128)} %fusion.4) | copy-start | bytes 1572868
  336.4 242.5 %collective-permute-start.1 = (bf16[2,128,256]{2,1,0:T(8,128)(2,1)}, bf16[2,128,256]{2,1,0:T(8,128)(2,1)}, u32[]{:S(2)}, u32[]{:S(2)}) collective-permute-start(bf16[2,128,256]{2,1,0:T(8,128)(2,1)} %fusion.50), channel_id=1, source_target_pairs={{1,0},{2,1},{3,2},{5,4},{6,5},{7,6},{9,8},{10,9},{11,10},{13,12},{... | collective-permute-start | bytes 393224 | tf_op jit(solution)/shard_map/ppermute | solution.py:13
  592.1 2.3 copy-start.4
  594.4 1.0 copy-start.15
  594.4 2.7 copy-start.20
  (2 other events, 1.4 us)
Sparse Core Ops, SparseCore 0:
  337.6 239.8 all-reduce.2
where the time goes:
time: 688 us; the launch traced here: 681 us
  waiting for transfers between devices  286 us (42%)
  other arithmetic  183 us (27%)
  blocking collectives  75 us (11%)
  local copies, waits for them, and re-layouts  58.8 us (9%)
  starting transfers between devices  45.2 us (7%)
  matrix products  18.1 us (3%)
  between operations  14.7 us (2%)
    psum x1, waiting for transfers between devices, body(): lax.psum((grad_conv_w, grad_conv_b, grad_mix_w, grad_mix_b), ('dp', 'spac...  237 us
    scatter-add x2, other arithmetic, back_finish(): total.at[:, :, send_rows[0]].add(returned * live_slots.astype(jnp.float32))  143 us
    psum x1, blocking collectives, body(): lax.psum((grad_conv_w, grad_conv_b, grad_mix_w, grad_mix_b), ('dp', 'spac...  75 us
    unnamed x63, local copies, waits for them, and re-layouts  26.4 us
    all_to_all x1, waiting for transfers between devices, body(): lax.all_to_all(packed_one, 'space', split_axis=2, concat_axis=2, tiled=True)  21.2 us
    all_to_all x1, waiting for transfers between devices, body(): lax.all_to_all(back_start(back_two, adj_tiles, tile_cols, send_rows), 'sp...  18.7 us
  transfers between devices with their start and end apart: 7, of which 5 were waited for; matrix products, arithmetic and copies ran while one was open for 3% of the time, Pallas kernels for 0%

commit v1 on v0

--- a/solution.py
+++ b/solution.py
@@ -174,8 +174,9 @@
         ]
     )
     grad_conv_b = jnp.sum(backward_preactivation.astype(jnp.float32), axis=(0, 2))
-    grad_conv_w, grad_conv_b, grad_mix_w, grad_mix_b = lax.psum(
-        (grad_conv_w, grad_conv_b, grad_mix_w, grad_mix_b), ("dp", "space", "tm")
+    knots_process = lambda xs: lax.psum(lax.psum(xs, axis_name="dp"), axis_name=("space", "tm"))
+    grad_conv_w, grad_conv_b, grad_mix_w, grad_mix_b = knots_process(
+        (grad_conv_w, grad_conv_b, grad_mix_w, grad_mix_b)
     )
     cell_count = (
         inputs.shape[0]

time: 688 us -> 909 us (1.32)
  the two profiles are of different devices: /device:TPU:1 before, /device:TPU:32 now
where the time goes in v1:
time: 909 us; the launch traced here: 901 us
  blocking collectives  322 us (35%)
  waiting for transfers between devices  278 us (31%)
  other arithmetic  183 us (20%)
  local copies, waits for them, and re-layouts  58.6 us (6%)
  starting transfers between devices  27.6 us (3%)
  matrix products  17.3 us (2%)
  between operations  14.7 us (2%)
    psum x1, blocking collectives, body(): lax.psum(lax.psum(xs, axis_name='dp'), axis_name=('space', 'tm'))  304 us
    psum x1, waiting for transfers between devices, body(): lax.psum(lax.psum(xs, axis_name='dp'), axis_name=('space', 'tm'))  168 us
    scatter-add x2, other arithmetic, back_finish(): total.at[:, :, send_rows[0]].add(returned * live_slots.astype(jnp.float32))  143 us
    psum x1, waiting for transfers between devices, body(): lax.psum(xs, axis_name='dp')  46.1 us
    unnamed x69, local copies, waits for them, and re-layouts  26.4 us
    all_to_all x1, waiting for transfers between devices, body(): lax.all_to_all(packed_one, 'space', split_axis=2, concat_axis=2, tiled=True)  23.3 us
    all_to_all x1, waiting for transfers between devices, body(): lax.all_to_all(back_start(back_two, adj_tiles, tile_cols, send_rows), 'sp...  22.2 us
    all_to_all x1, waiting for transfers between devices, body(): lax.all_to_all(back_start(back_one, adj_tiles, tile_cols, send_rows), 'sp...  18.7 us
  transfers between devices with their start and end apart: 8, of which 5 were waited for; matrix products, arithmetic and copies ran while one was open for 2% of the time, Pallas kernels for 0%

profile of v1, /device:TPU:32, one launch (start us, length us, event | category | flops | bytes accessed | tf_op | source)
XLA Modules:
  0.0 901.4 jit_solution(8544538356201334967)
XLA Ops:
  12.5 3.5 scatter_fusion.1
  19.6 8.7 all-to-all-start.2
  31.9 22.2 %all-to-all-done.2 = bf16[16,2,16384]{2,1,0:T(2,128)(2,1)} async-done(((bf16[16,2,16384]{2,1,0:T(2,128)(2,1)}), bf16[16,2,16384]{2,1,0:T(2,128)(2,1)}, u32[]{:S(2)}, u32[]{:S(2)}) %all-to-all-start.2) | async-done | bytes 1048608 | tf_op jit(solution)/shard_map/all_to_all | solution.py:116
  54.1 3.8 reshape.259
  57.8 3.1 convert_multiply_fusion.1
  61.0 71.3 %scatter_fusion.2 = f32[8,64,256]{1,0,2:T(8,128)S(1)} fusion(f32[8,64,256]{1,0,2:T(8,128)S(1)} %copy.84, s32[1024]{0:T(1024)S(1)} %reshape.131, f32[1024,8,64]{2,1,0:T(8,128)} %bitcast.273), kind=kCustom, calls=%fused_computation.6 | custom fusion | flops 524288 | bytes 6295552 | tf_op jit(solution)/shard_map/scatter-add | solution.py:73
  135.4 3.5 scatter_fusion.4
  144.5 5.3 all-to-all-start.3
  156.6 18.7 %all-to-all-done.3 = bf16[16,2,16384]{2,1,0:T(2,128)(2,1)} async-done(((bf16[16,2,16384]{2,1,0:T(2,128)(2,1)}), bf16[16,2,16384]{2,1,0:T(2,128)(2,1)}, u32[]{:S(2)}, u32[]{:S(2)}) %all-to-all-start.3) | async-done | bytes 1048608 | tf_op jit(solution)/shard_map/all_to_all | solution.py:127
  175.3 3.8 reshape.261
  179.1 3.1 convert_multiply_fusion
  182.2 71.3 %scatter_fusion.5 = f32[8,64,256]{1,0,2:T(8,128)S(1)} fusion(f32[8,64,256]{1,0,2:T(8,128)S(1)} %copy.92, s32[1024]{0:T(1024)S(1)} %reshape.131, f32[1024,8,64]{2,1,0:T(8,128)} %bitcast.272), kind=kCustom, calls=%fused_computation.9 | custom fusion | flops 524288 | bytes 6295552 | tf_op jit(solution)/shard_map/scatter-add | solution.py:73
  255.7 7.6 gather_fusion
  263.3 4.9 fusion.76
  270.5 5.2 all-to-all-start
  277.2 23.3 %all-to-all-done = bf16[16,2,16384]{2,1,0:T(2,128)(2,1)S(1)} async-done(((bf16[16,2,16384]{2,1,0:T(2,128)(2,1)}), bf16[16,2,16384]{2,1,0:T(2,128)(2,1)S(1)}, u32[]{:S(2)}, u32[]{:S(2)}) %all-to-all-start) | async-done | bytes 1048608 | tf_op jit(solution)/shard_map/all_to_all | solution.py:106
  300.5 2.3 reshape.255
  302.8 3.4 pad_maximum_fusion
  306.2 3.3 copy.65
  309.5 2.3 gather_fusion.1
  312.9 3.3 gather_fusion.2
  316.2 4.8 fusion.77
  321.0 4.7 reshape.256
  325.7 5.3 all-to-all-start.1
  334.6 46.1 %all-reduce.5.cloned.1.call-done = f32[2,128,64]{1,2,0:T(8,128)} async-done(((f32[2,128,64]{1,2,0:T(8,128)}), f32[2,128,64]{1,2,0:T(8,128)}) %all-reduce.5.cloned.1.call-update) | async-done | bytes 65552 | tf_op jit(solution)/shard_map/psum | solution.py:177
  383.2 168.0 %all-reduce.7.cloned.1.call-done = f32[2,128,64]{1,2,0:T(8,128)} async-done(((f32[2,128,64]{1,2,0:T(8,128)}), f32[2,128,64]{1,2,0:T(8,128)}) %all-reduce.7.cloned.1.call-update) | async-done | bytes 65552 | tf_op jit(solution)/shard_map/psum | solution.py:177
  556.7 2.3 reshape.257
  559.0 3.4 pad_maximum_fusion.1
  562.4 3.3 copy.71
  565.7 2.3 gather_fusion.3
  570.8 18.1 %all-reduce.1 = (f32[128]{0:T(128)S(1)}, f32[3,64,64]{1,2,0:T(8,128)S(1)}, f32[64]{0:T(128)S(1)}) all-reduce(f32[128]{0:T(128)S(1)} %convert_reduce_fusion, f32[3,64,64]{1,2,0:T(8,128)S(1)} %pad_maximum_fusion.6, f32[64]{0:T(128)S(1)} %convert_reduce_fusion.1), channel_id=1, replica_groups=mesh['dp'=4,'space'=16,'tm'=4] {'dp'}, use_global_device_ids=true, to_apply=%region_9.0 | all-reduce | flops 12480 | bytes 99840 | tf_op jit(solution)/shard_map/psum | solution.py:177
  588.9 303.9 %all-reduce = (f32[128]{0:T(128)S(1)}, f32[3,64,64]{1,2,0:T(8,128)S(1)}, f32[64]{0:T(128)S(1)}) all-reduce(f32[128]{0:T(128)S(1)} %get-tuple-element.27, f32[3,64,64]{1,2,0:T(8,128)S(1)} %get-tuple-element.28, f32[64]{0:T(128)S(1)} %get-tuple-element.29), channel_id=1, replica_groups=mesh['dp'=4,'space'=16,'tm'=4] {'space','tm'}, use_global_device_ids=true, to_apply=%region_10.0 | all-reduce | flops 12480 | bytes 99840 | tf_op jit(solution)/shard_map/psum | solution.py:177
  (145 shorter events, 50.8 us)
Async XLA Ops:
  17.3 11.0 %copy-start.1 = (bf16[2,8,128,128]{3,2,1,0:T(8,128)(2,1)S(1)}, bf16[2,8,128,128]{3,2,1,0:T(8,128)(2,1)}, u32[]{:S(2)}) copy-start(bf16[2,8,128,128]{3,2,1,0:T(8,128)(2,1)} %param.16) | copy-start | bytes 1572868
  19.6 34.5 %all-to-all-start.2 = ((bf16[16,2,16384]{2,1,0:T(2,128)(2,1)}), bf16[16,2,16384]{2,1,0:T(2,128)(2,1)}, u32[]{:S(2)}, u32[]{:S(2)}) async-start(bf16[16,2,16384]{2,1,0:T(2,128)(2,1)} %reshape.258), calls=%async_computation.2 | async-start | bytes 2097152 | tf_op jit(solution)/shard_map/all_to_all | solution.py:116
  29.0 1.9 copy-start
  29.1 1.9 copy-start.19
  142.2 7.5 copy-start.12
  144.5 7.1 copy-start.21
  144.5 7.5 copy-start.29
  144.5 30.8 %all-to-all-start.3 = ((bf16[16,2,16384]{2,1,0:T(2,128)(2,1)}), bf16[16,2,16384]{2,1,0:T(2,128)(2,1)}, u32[]{:S(2)}, u32[]{:S(2)}) async-start(bf16[16,2,16384]{2,1,0:T(2,128)(2,1)} %reshape.260), calls=%async_computation.3 | async-start | bytes 2097152 | tf_op jit(solution)/shard_map/all_to_all | solution.py:127
  149.8 2.2 collective-permute-start
  151.6 1.7 copy-start.17
  152.0 1.3 copy-start.22
  255.0 21.2 %copy-start.5 = (bf16[8,64,256]{2,1,0:T(8,128)(2,1)}, bf16[8,64,256]{2,1,0:T(8,128)(2,1)S(1)}, u32[]{:S(2)}) copy-start(bf16[8,64,256]{2,1,0:T(8,128)(2,1)S(1)} %get-tuple-element.30) | copy-start | bytes 786436
  255.0 21.2 %copy-start.7 = (bf16[8,64,256]{2,1,0:T(8,128)(2,1)}, bf16[8,64,256]{2,1,0:T(8,128)(2,1)S(1)}, u32[]{:S(2)}) copy-start(bf16[8,64,256]{2,1,0:T(8,128)(2,1)S(1)} %get-tuple-element.31) | copy-start | bytes 786436
  268.2 7.5 copy-start.25
  270.5 5.5 copy-start.18
  270.5 5.5 copy-start.23
  270.5 5.8 copy-start.13
  270.5 30.0 %all-to-all-start = ((bf16[16,2,16384]{2,1,0:T(2,128)(2,1)}), bf16[16,2,16384]{2,1,0:T(2,128)(2,1)S(1)}, u32[]{:S(2)}, u32[]{:S(2)}) async-start(bf16[16,2,16384]{2,1,0:T(2,128)(2,1)} %reshape.254), calls=%async_computation | async-start | bytes 2097152 | tf_op jit(solution)/shard_map/all_to_all | solution.py:106
  309.5 2.3 copy-start.3
  321.0 10.0 %copy-start.24 = (f32[1,128,64]{1,2,0:T(8,128)S(1)}, f32[1,128,64]{1,2,0:T(8,128)}, u32[]{:S(2)}) copy-start(f32[1,128,64]{1,2,0:T(8,128)} %convolution_bitcast_fusion.13) | copy-start | bytes 98308
  321.0 10.7 %copy-start.10 = (bf16[8,64,256]{2,1,0:T(8,128)(2,1)S(1)}, bf16[8,64,256]{2,1,0:T(8,128)(2,1)}, u32[]{:S(2)}) copy-start(bf16[8,64,256]{2,1,0:T(8,128)(2,1)} %copy-done.9) | copy-start | bytes 786436
  325.7 6.9 copy-start.6
  325.7 6.9 copy-start.8
  325.7 7.9 copy-start.14
  325.7 7.9 copy-start.28
  325.7 231.0 %all-to-all-start.1 = ((bf16[16,2,16384]{2,1,0:T(2,128)(2,1)}), bf16[16,2,16384]{2,1,0:T(2,128)(2,1)S(1)}, u32[]{:S(2)}, u32[]{:S(2)}) async-start(bf16[16,2,16384]{2,1,0:T(2,128)(2,1)} %reshape.256), calls=%async_computation.1 | async-start | bytes 2097152 | tf_op jit(solution)/shard_map/all_to_all | solution.py:109
  331.0 49.8 %all-reduce.5.cloned.1.call-start = ((), (), s32[]{:S(2)}) async-start(), calls=%async_computation.4 | async-start | bytes 131072 | tf_op jit(solution)/shard_map/psum | solution.py:177
  331.7 219.5 %all-reduce.7.cloned.1.call-start = ((), (), s32[]{:S(2)}) async-start(), calls=%async_computation.5 | async-start | bytes 131072 | tf_op jit(solution)/shard_map/psum | solution.py:177
  334.6 220.4 %copy-start.16 = (f32[8,64,256]{2,1,0:T(8,128)S(1)}, f32[8,64,256]{2,1,0:T(8,128)}, u32[]{:S(2)}) copy-start(f32[8,64,256]{2,1,0:T(8,128)} %fusion.4) | copy-start | bytes 1572868
  381.4 171.2 %collective-permute-start.1 = (bf16[2,128,256]{2,1,0:T(8,128)(2,1)}, bf16[2,128,256]{2,1,0:T(8,128)(2,1)}, u32[]{:S(2)}, u32[]{:S(2)}) collective-permute-start(bf16[2,128,256]{2,1,0:T(8,128)(2,1)} %fusion.50), channel_id=1, source_target_pairs={{1,0},{2,1},{3,2},{5,4},{6,5},{7,6},{9,8},{10,9},{11,10},{13,12},{... | collective-permute-start | bytes 393224 | tf_op jit(solution)/shard_map/ppermute | solution.py:13
  565.7 2.3 copy-start.4
  568.1 2.7 copy-start.20
  (6 other events, 5.5 us)
Sparse Core Ops, SparseCore 0:
  334.7 46.0 all-reduce.4
  384.6 166.5 all-reduce.6
